TPU v7x, 32 devices: a whole 2x2x4 slice. The times are simulated.
32 devices in a mesh: ctx: 16 (over z, y, x), dp: 2 (over core).
Axes of the slice: x: 2, y: 2, z: 4, core: 2. Of those that a mesh axis runs over, the one named last changes fastest.
Arguments:
- inputs: bfloat16 [2, 2048, 12288], P('dp', 'ctx'), may hold values from -6 to 6
- feat_weight: float32 [7, 12288], P(None, 'dp'), may hold values from -2 to 2
- filter_taps: float32 [128, 4096], P(None, 'dp'), may hold values from -0.5 to 0.5
- upstream: bfloat16 [2, 2048, 4096], P('dp', 'ctx'), may hold values from -6 to 6
Outputs:
- filter_grad: float32 [128, 4096], P(None, 'dp')
- feat_grad: float32 [7, 12288], P(None, 'dp')
All inputs are finite; a program needn't handle non-finite values.
Results may differ from a plain program's by a relative error of at most 0.0041.
Values may be sent and summed in bfloat16 or wider, within the bound.
A program may use at most 128 MiB of HBM per device.

v0:
```python
import functools

import jax
import jax.numpy as jnp
import numpy as np
from jax import lax
from jax.experimental import pallas as pl
from jax.experimental.pallas import tpu as pltpu
from jax.sharding import PartitionSpec as P

PAD = 8
F32 = jnp.float32
BF16 = jnp.bfloat16


def from_behind(block, axis, distance):
    devices = range(lax.axis_size(axis))
    route = [(i - distance, i) for i in devices if i - distance in devices]
    return lax.ppermute(block, axis, route)


def two_parts(matrix):
    high = matrix.astype(BF16)
    low = (matrix - high.astype(np.float64)).astype(BF16)
    return high, low


def transforms(rows, taps):
    size = rows + taps
    half = size // 2
    angle = 2 * np.pi * np.outer(np.arange(half), np.arange(size)) / size
    cosines = np.cos(angle)
    sines = -np.sin(angle)
    sines[0] = np.cos(np.pi * np.arange(size))
    forward = np.concatenate([cosines, sines], 0)
    weight = np.full((size, 1), 2.0 / size)
    weight[0] = weight[half] = 1.0 / size
    backward = (forward * weight).T
    f_high, f_low = two_parts(forward)
    b_high, b_low = two_parts(backward)
    cat = lambda *parts: np.concatenate(parts, 1)
    return (
        cat(f_high[:, :rows], f_low[:, :rows]),
        cat(f_high[:, :taps], f_low[:, :taps], f_high[:, :taps]),
        cat(f_high, f_low),
        cat(b_high, b_low),
    )


def dot(a, b):
    return jnp.dot(a, b, preferred_element_type=F32)


def chunk_terms(q_ext, k_ext, v_ext, up_ext, taps, weights, mats, rows, reach):
    to_mixed, to_taps, to_grad, back = mats
    size = up_ext.shape[0]
    half = size // 2

    def featured(ext, w, out_rows):
        total = w[0:1] * ext[PAD : PAD + out_rows, :]
        for j in range(1, reach):
            total += w[j : j + 1] * ext[PAD - j : PAD - j + out_rows, :]
        return total

    def lagged(grad, ext, out_rows):
        sums = [
            jnp.sum(grad * ext[PAD - j : PAD - j + out_rows, :], 0, keepdims=True)
            for j in range(reach)
        ]
        sums += [jnp.zeros_like(sums[0])] * (PAD - reach)
        return jnp.concatenate(sums, 0)

    key_part = featured(k_ext, weights[1], rows)
    value_part = featured(v_ext, weights[2], rows)
    mixed = (key_part * value_part).astype(BF16)
    m_hat = dot(to_mixed[...], jnp.concatenate([mixed, mixed], 0))
    taps_high = taps.astype(BF16)
    taps_low = (taps - taps_high.astype(F32)).astype(BF16)
    t_hat = dot(to_taps[...], jnp.concatenate([taps_high, taps_high, taps_low], 0))
    query = featured(q_ext, weights[0], size)
    grad_conv = (up_ext[...].astype(F32) * query).astype(BF16)
    g_hat = dot(to_grad[...], jnp.concatenate([grad_conv, grad_conv], 0))

    m_re, m_im = m_hat[:half], m_hat[half:]
    t_re, t_im = t_hat[:half], t_hat[half:]
    g_re, g_im = g_hat[:half], g_hat[half:]
    first = lax.broadcasted_iota(jnp.int32, m_re.shape, 0) == 0
    t_imz = jnp.where(first, 0.0, t_im)
    t_ren = jnp.where(first, t_im, t_re)
    m_imz = jnp.where(first, 0.0, m_im)
    m_ren = jnp.where(first, m_im, m_re)

    def inverse(re, im, out_rows):
        re, im = re.astype(BF16), im.astype(BF16)
        return dot(back[:out_rows, :], jnp.concatenate([re, im, re, im], 0))

    conv_out = inverse(
        m_re * t_re - m_im * t_imz, m_re * t_imz + m_im * t_ren, size
    )
    grad_mixed = inverse(
        g_re * t_re + g_im * t_imz, g_im * t_ren - g_re * t_imz, rows
    )
    filter_part = inverse(
        g_re * m_re + g_im * m_imz, g_im * m_ren - g_re * m_imz, taps.shape[0]
    )
    return (
        filter_part,
        lagged(up_ext[...].astype(F32) * conv_out, q_ext, size),
        lagged(grad_mixed * value_part, k_ext, rows),
        lagged(grad_mixed * key_part, v_ext, rows),
    )


def local_kernel(
    reach, xq, xk, xv, pq, pk, pv, nq, up, nup, taps, wq, wk, wv, m0, m1, m2, m3,
    filt, fq, fk, fv, q_ext, k_ext, v_ext, up_ext,
):
    rows = xq.shape[0]
    size = up_ext.shape[0]
    for ext, prev, block in ((q_ext, pq, xq), (k_ext, pk, xk), (v_ext, pv, xv)):
        ext[0:PAD, :] = prev[...].astype(F32)
        ext[PAD : PAD + rows, :] = block[...].astype(F32)
    q_ext[PAD + rows : PAD + size, :] = nq[...].astype(F32)
    up_ext[0:rows, :] = up[...]
    up_ext[rows:size, :] = nup[...]
    filt[...], fq[...], fk[...], fv[...] = chunk_terms(
        q_ext, k_ext, v_ext, up_ext, taps[...], (wq[...], wk[...], wv[...]),
        (m0, m1, m2, m3), rows, reach,
    )


def by_collectives(inputs, feat_weight, filter_taps, upstream):
    inputs_here = inputs[0]
    grad_here = upstream[0]
    rows = inputs_here.shape[0]
    channels = grad_here.shape[1]
    filt_rows = filter_taps.shape[0]
    reach = feat_weight.shape[0]
    scale = (lax.axis_size("dp") * lax.axis_size("ctx") * rows) ** (-0.5)
    feat_full, taps_full = (
        lax.all_gather(feat_weight, "dp", axis=1, tiled=True),
        lax.all_gather(filter_taps, "dp", axis=1, tiled=True),
    )
    next_grad, next_query = from_behind(
        (grad_here[:filt_rows], inputs_here[:filt_rows, :channels]), "ctx", -1
    )
    before = from_behind(inputs_here[rows - PAD :], "ctx", 1)
    weights = jnp.concatenate(
        [feat_full, jnp.zeros((PAD - reach, feat_full.shape[1]), F32)], 0
    )
    mats = [jnp.asarray(m) for m in transforms(rows, filt_rows)]
    width = 256
    steps = channels // width
    size = rows + filt_rows
    part = lambda r, group: pl.BlockSpec((r, width), lambda i: (0, i + group * steps))
    whole = lambda m: pl.BlockSpec(m.shape, lambda i: (0, 0))
    out = lambda r: jax.ShapeDtypeStruct((r, channels), F32)
    filter_part, feat_q, feat_k, feat_v = pl.pallas_call(
        functools.partial(local_kernel, reach),
        grid=(steps,),
        out_shape=[out(filt_rows), out(PAD), out(PAD), out(PAD)],
        in_specs=[part(rows, g) for g in range(3)]
        + [part(PAD, g) for g in range(3)]
        + [part(filt_rows, 0), part(rows, 0), part(filt_rows, 0), part(filt_rows, 0)]
        + [part(PAD, g) for g in range(3)]
        + [whole(m) for m in mats],
        out_specs=[part(filt_rows, 0)] + [part(PAD, 0)] * 3,
        scratch_shapes=[
            pltpu.VMEM((PAD + size, width), F32),
            pltpu.VMEM((PAD + rows, width), F32),
            pltpu.VMEM((PAD + rows, width), F32),
            pltpu.VMEM((size, width), BF16),
        ],
    )(
        inputs_here, inputs_here, inputs_here, before, before, before, next_query,
        grad_here, next_grad, taps_full, weights, weights, weights, *mats,
    )
    feat_part = jnp.concatenate([feat_q, feat_k, feat_v], 1)[:reach]
    filter_summed, feat_summed = (
        lax.psum_scatter(filter_part, "dp", scatter_dimension=1, tiled=True),
        lax.psum_scatter(feat_part, "dp", scatter_dimension=1, tiled=True),
    )
    filter_whole, feat_whole = lax.psum((filter_summed, feat_summed), "ctx")
    return (filter_whole * scale, feat_whole * scale)


MESH = pl.DeviceIdType.MESH
LANES = 128
GROUP = 2
PLANE = 4


def fused_kernel(
    reach, scale, x, up, taps_here, w_here, m0, m1, m2, m3, filt_out, feat_out,
    taps_all, w_all, tail, prev, n_up, n_q, r_up, r_q, q_ext, k_ext, v_ext, up_ext,
    stage, dp_got, rs_send, rs_got, gathered,
    own_sem, swap_send, swap_got, tail_send, tail_got, halo_send, halo_got,
    relay_send, relay_got,
    dp_send, dp_recv, rs_ssem, rs_rsem, ag_ssem, ag_rsem,
):
    n = lax.axis_size("ctx")
    me, core = lax.axis_index("ctx"), lax.axis_index("dp")
    rows, filt_rows = x.shape[0], taps_here.shape[0]
    channels = up.shape[1]
    half = channels // 2
    feat_half = w_here.shape[1]
    size = rows + filt_rows
    packed = stage.shape[2]
    partner = {"dp": 1 - core}

    barrier = pltpu.get_barrier_semaphore()
    pl.semaphore_signal(barrier, inc=1, device_id=partner, device_id_type=MESH)

    @pl.loop(1, n)
    def _(j):
        pl.semaphore_signal(
            barrier, inc=1, device_id={"ctx": lax.rem(me + j, n)}, device_id_type=MESH
        )

    def remote(src, dst, send, got, device):
        return pltpu.make_async_remote_copy(
            src_ref=src, dst_ref=dst, send_sem=send, recv_sem=got,
            device_id=device, device_id_type=MESH,
        )

    def lanes_of(owner, piece):
        return pl.ds(pl.multiple_of(owner * LANES + piece * half, LANES), LANES)

    def swaps():
        taps_side = pl.ds(pl.multiple_of(core * half, LANES), half)
        feat_side = pl.ds(pl.multiple_of(core * feat_half, LANES), feat_half)
        return (
            remote(taps_here, taps_all.at[:, taps_side], swap_send.at[0], swap_got.at[0], partner),
            remote(w_here, w_all.at[:, feat_side], swap_send.at[1], swap_got.at[1], partner),
        ), (
            pltpu.make_async_copy(taps_here, taps_all.at[:, taps_side], own_sem.at[0]),
            pltpu.make_async_copy(w_here, w_all.at[:, feat_side], own_sem.at[1]),
        )

    def tail_copy():
        return remote(tail, prev, tail_send, tail_got, {"ctx": lax.rem(me + 1, n)})

    groups = n // GROUP

    def block_copies(g, first, sources, targets, send, got, device):
        copies = []
        for piece in range(2):
            low = first * (GROUP * LANES) + piece * half
            at = pl.ds(pl.multiple_of(low, LANES), GROUP * LANES)
            for k, (src, dst) in enumerate(zip(sources, targets)):
                s = 2 * piece + k
                copies.append(
                    remote(
                        src.at[pl.ds(0, filt_rows), at], dst.at[:, at],
                        send.at[g, s], got.at[g, s], {"ctx": device},
                    )
                )
        return copies

    head, landing, relay = (up, x), (n_up, n_q), (r_up, r_q)
    near = (me > 0) & (lax.rem(me, PLANE) != 0)
    far = (me > 0) & (lax.rem(me, PLANE) == 0)
    relays = (lax.rem(me, PLANE) == 0) & (me < n - PLANE)

    def near_copies(g):
        back = lax.rem(me + n - 1, n)
        return block_copies(
            g, group_at(g, back), head, landing, halo_send, halo_got, back
        )

    def far_copies(g):
        back = lax.rem(me + n - 1, n)
        via = lax.rem(me + n - PLANE, n)
        return block_copies(g, group_at(g, back), head, relay, halo_send, relay_got, via)

    def arrivals(g):
        return block_copies(
            g, group_at(g, me), head, landing, halo_send, halo_got, lax.rem(me + 1, n)
        )

    def relay_arrivals(g):
        end = lax.rem(me + PLANE - 1, n)
        return block_copies(
            g, group_at(g, end), head, relay, halo_send, relay_got, lax.rem(me + PLANE, n)
        )

    def relay_copies(g):
        end = lax.rem(me + PLANE - 1, n)
        return block_copies(
            g, group_at(g, end), relay, landing, relay_send, halo_got, end
        )

    def group_at(g, device):
        return lax.rem(g + 1 + device // GROUP, groups)

    sent, kept = swaps()
    for copy in kept:
        copy.start()

    tail[...] = x[rows - PAD :, :]

    @pl.when(me == 0)
    def _():
        prev[...] = jnp.zeros_like(prev)

    @pl.when(me == n - 1)
    def _():
        n_up[...] = jnp.zeros_like(n_up)
        n_q[...] = jnp.zeros_like(n_q)

    pl.semaphore_wait(barrier, n)
    for copy in sent:
        copy.start()

    @pl.when(me < n - 1)
    def _():
        tail_copy().start()

    @pl.when(near)
    def _():
        @pl.loop(0, groups)
        def _(g):
            for copy in near_copies(g):
                copy.start()

    @pl.when(far)
    def _():
        @pl.loop(0, groups)
        def _(g):
            for copy in far_copies(g):
                copy.start()

    for copy in kept:
        copy.wait()
    for copy in sent:
        copy.wait()

    @pl.when(me > 0)
    def _():
        tail_copy().wait_recv()

    def dp_copy(i):
        return remote(
            stage.at[i, 1 - core], dp_got.at[i], dp_send.at[i], dp_recv.at[i], partner
        )

    def rs_copy(i, owner):
        return remote(
            rs_send.at[i], rs_got.at[me], rs_ssem.at[i], rs_rsem.at[me], {"ctx": owner}
        )

    def owner_at(i):
        return group_at(i // GROUP, me) * GROUP + lax.rem(i + 1 + me, GROUP)

    def compute(i):
        owner = owner_at(i)

        @pl.when(relays & (lax.rem(i, GROUP) == 0))
        def _():
            g = i // GROUP
            for came, goes in zip(relay_arrivals(g), relay_copies(g)):
                came.wait_recv()
                goes.start()

        @pl.when((me < n - 1) & (lax.rem(i, GROUP) == 0))
        def _():
            for copy in arrivals(i // GROUP):
                copy.wait_recv()

        def both(ref, group):
            return jnp.concatenate(
                [ref[:, pl.ds(pl.multiple_of(group * channels + p * half + owner * LANES, LANES), LANES)] for p in range(2)],
                1,
            )

        for group, ext in enumerate((q_ext, k_ext, v_ext)):
            ext[0:PAD, :] = both(prev, group).astype(F32)
            ext[PAD : PAD + rows, :] = both(x, group).astype(F32)
        q_ext[PAD + rows : PAD + size, :] = both(n_q, 0).astype(F32)
        up_ext[0:rows, :] = both(up, 0)
        up_ext[rows:size, :] = both(n_up, 0)
        filt, feat_q, feat_k, feat_v = chunk_terms(
            q_ext, k_ext, v_ext, up_ext, both(taps_all, 0),
            [both(w_all, group) for group in range(3)],
            (m0, m1, m2, m3), rows, reach,
        )
        a, b = slice(0, LANES), slice(LANES, 2 * LANES)
        rest = [jnp.zeros((packed - filt_rows - 3 * PAD, LANES), F32)]
        stage[i, 0] = jnp.concatenate(
            [filt[:, a], feat_q[:, a], feat_q[:, b], feat_k[:, a]] + rest, 0
        )
        stage[i, 1] = jnp.concatenate(
            [filt[:, b], feat_k[:, b], feat_v[:, a], feat_v[:, b]] + rest, 0
        )
        dp_copy(i).start()

    def reduce_pair(i):
        dp_copy(i).wait_recv()
        return (stage[i, core] + dp_got[i]).astype(BF16)

    def send_on(i):
        rs_send[i] = reduce_pair(i)
        rs_copy(i, owner_at(i)).start()

    @pl.loop(0, n)
    def _(i):
        compute(i)

        @pl.when(i > 0)
        def _():
            send_on(i - 1)

    total = reduce_pair(n - 1).astype(F32)
    for j in range(1, n):
        src = lax.rem(me + j, n)
        remote(
            rs_send.at[0], rs_got.at[src], rs_ssem.at[0], rs_rsem.at[src], {"ctx": src}
        ).wait_recv()
        total += rs_got[src].astype(F32)
    gathered[me] = total.astype(BF16)

    planes = n // PLANE

    def ag_copy(k, q):
        owner = lax.rem(me + k * PLANE, n)
        target = me // PLANE * PLANE + lax.rem(me + q, PLANE)
        return remote(
            gathered.at[owner], gathered.at[owner], ag_ssem.at[k, q], ag_rsem.at[owner],
            {"ctx": target},
        )

    def ag_column(k):
        return remote(
            gathered.at[me], gathered.at[me], ag_ssem.at[k, 0], ag_rsem.at[me],
            {"ctx": lax.rem(me + k * PLANE, n)},
        )

    def ag_arrival(owner):
        return remote(
            gathered.at[owner], gathered.at[owner], ag_ssem.at[0, 0], ag_rsem.at[owner],
            {"ctx": lax.rem(me + 1, n)},
        )

    @pl.loop(1, planes)
    def _(k):
        ag_column(k).start()

    @pl.loop(1, PLANE)
    def _(q):
        ag_copy(0, q).start()

    def unpack(owner):
        value = gathered[owner].astype(F32) * scale
        filt_out[:, pl.ds(pl.multiple_of(owner * LANES, LANES), LANES)] = value[:filt_rows]
        for g in range(3):
            low = filt_rows + g * PAD
            at = pl.ds(pl.multiple_of(owner * LANES + g * half, LANES), LANES)
            feat_out[:, at] = value[low : low + reach]

    unpack(me)

    @pl.loop(1, planes)
    def _(k):
        src = lax.rem(me + k * PLANE, n)
        ag_arrival(src).wait_recv()

        @pl.loop(1, PLANE)
        def _(q):
            ag_copy(k, q).start()

        unpack(src)

    @pl.loop(0, planes)
    def _(k):
        @pl.loop(1, PLANE)
        def _(q):
            low = lax.rem(me // PLANE + k, planes) * PLANE
            src = low + lax.rem(me + q, PLANE)
            ag_arrival(src).wait_recv()
            unpack(src)

    @pl.when(me < n - 1)
    def _():
        tail_copy().wait_send()

    @pl.when(near)
    def _():
        @pl.loop(0, groups)
        def _(g):
            for copy in near_copies(g):
                copy.wait_send()

    @pl.when(far)
    def _():
        @pl.loop(0, groups)
        def _(g):
            for copy in far_copies(g):
                copy.wait_send()

    @pl.when(relays)
    def _():
        @pl.loop(0, groups)
        def _(g):
            for copy in relay_copies(g):
                copy.wait_send()

    @pl.loop(0, n)
    def _(i):
        dp_copy(i).wait_send()

    @pl.loop(0, n - 1)
    def _(i):
        rs_copy(i, owner_at(i)).wait_send()

    @pl.loop(1, planes)
    def _(k):
        ag_column(k).wait_send()

    @pl.loop(0, planes)
    def _(k):
        @pl.loop(1, PLANE)
        def _(q):
            ag_copy(k, q).wait_send()


def fused(inputs, feat_weight, filter_taps, upstream):
    x, up = inputs[0], upstream[0]
    n = lax.axis_size("ctx")
    rows, channels = up.shape
    filt_rows, reach = filter_taps.shape[0], feat_weight.shape[0]
    scale = (lax.axis_size("dp") * n * rows) ** (-0.5)
    mats = [jnp.asarray(m) for m in transforms(rows, filt_rows)]
    size = rows + filt_rows
    width = 2 * LANES
    packed = -(-(filt_rows + 3 * PAD) // 16) * 16
    dma = lambda *shape: pltpu.SemaphoreType.DMA(shape)
    return pl.pallas_call(
        functools.partial(fused_kernel, reach, scale),
        out_shape=[
            jax.ShapeDtypeStruct(filter_taps.shape, F32),
            jax.ShapeDtypeStruct(feat_weight.shape, F32),
        ],
        in_specs=[pl.BlockSpec(memory_space=pltpu.VMEM)] * 8,
        out_specs=[pl.BlockSpec(memory_space=pltpu.VMEM)] * 2,
        scratch_shapes=[
            pltpu.VMEM((filt_rows, channels), F32),
            pltpu.VMEM((reach, x.shape[1]), F32),
            pltpu.VMEM((PAD, x.shape[1]), BF16),
            pltpu.VMEM((PAD, x.shape[1]), BF16),
            pltpu.VMEM((filt_rows, channels), BF16),
            pltpu.VMEM((filt_rows, channels), BF16),
            pltpu.VMEM((filt_rows, channels), BF16),
            pltpu.VMEM((filt_rows, channels), BF16),
            pltpu.VMEM((PAD + size, width), F32),
            pltpu.VMEM((PAD + rows, width), F32),
            pltpu.VMEM((PAD + rows, width), F32),
            pltpu.VMEM((size, width), BF16),
            pltpu.VMEM((n, 2, packed, LANES), F32),
            pltpu.VMEM((n, packed, LANES), F32),
            pltpu.VMEM((n, packed, LANES), BF16),
            pltpu.VMEM((n, packed, LANES), BF16),
            pltpu.VMEM((n, packed, LANES), BF16),
            dma(2), dma(2), dma(2),
            pltpu.SemaphoreType.DMA, pltpu.SemaphoreType.DMA,
            *[dma(n // GROUP, 4)] * 4,
            dma(n), dma(n), dma(n), dma(n), dma(n // PLANE, PLANE), dma(n),
        ],
        compiler_params=pltpu.CompilerParams(
            collective_id=0, has_side_effects=True, vmem_limit_bytes=60 * 2**20
        ),
    )(x, up, filter_taps, feat_weight, *mats)


def per_device(inputs, feat_weight, filter_taps, upstream):
    n = lax.axis_size("ctx")
    cut = 2 * n * LANES
    whole = n % GROUP == 0 and n % PLANE == 0 and PLANE % GROUP == 0
    if lax.axis_size("dp") == 2 and upstream.shape[2] == cut and whole:
        return fused(inputs, feat_weight, filter_taps, upstream)
    return by_collectives(inputs, feat_weight, filter_taps, upstream)


def solution(mesh):
    placed = (P("dp", "ctx", None), P(None, "dp"), P(None, "dp"), P("dp", "ctx", None))
    return jax.shard_map(
        per_device,
        mesh=mesh,
        in_specs=placed,
        out_specs=(P(None, "dp"), P(None, "dp")),
        check_vma=False,
    )
```

profile of v0, /device:TPU:0, one launch (start us, length us, event | category | flops | bytes accessed | tf_op | source)
XLA Modules:
  0.0 96.9 jit_solution(4600832550120342596)
XLA Ops:
  0.6 92.4 %shard_map.95 = (f32[128,2048]{1,0:T(8,128)}, f32[7,6144]{1,0:T(8,128)}) custom-call(bf16[128,12288]{1,0:T(8,128)(2,1)} %bitcast.2, bf16[128,4096]{1,0:T(8,128)(2,1)} %bitcast.3, f32[128,2048]{1,0:T(8,128)} %taps_here.1, f32[7,6144]{1,0:T(8,128)} %w_here.1, bf16[256,256]{1,0:T(8,128)(2,1)} %constant.8.clone.m0, bf16[256,384]{1,0:T(8,128)(2,1)} %constant.9.clone.m1, ...), custom_call_target="tpu_custom_call" | custom-call | tf_op jit(solution)/shard_map/pallas_call | solution.py:537
  93.0 2.3 %copy.12 = f32[128,2048]{1,0:T(8,128)} copy(f32[128,2048]{1,0:T(8,128)} %get-tuple-element.4) | data formatting | bytes 2097152
  95.3 1.6 %copy.13 = f32[7,6144]{1,0:T(8,128)} copy(f32[7,6144]{1,0:T(8,128)} %get-tuple-element.5) | data formatting | bytes 344064
where the time goes:
time: 97.1 us; the launch traced here: 96.9 us
  Pallas kernels  92.4 us (95%)
  local copies, waits for them, and re-layouts  3.91 us (4%)
    pallas_call x1, Pallas kernels, fused(): pl.pallas_call(functools.partial(fused_kernel, reach, scale), out_shape=[...  92.4 us
    unnamed x2, local copies, waits for them, and re-layouts  3.91 us

commit v1 on v0

v1 whole, which is shorter than its diff:
```python
import functools

import jax
import jax.numpy as jnp
import numpy as np
from jax import lax
from jax.experimental import pallas as pl
from jax.experimental.pallas import tpu as pltpu
from jax.sharding import PartitionSpec as P

PAD = 8
F32 = jnp.float32
BF16 = jnp.bfloat16


def from_behind(block, axis, distance):
    devices = range(lax.axis_size(axis))
    route = [(i - distance, i) for i in devices if i - distance in devices]
    return lax.ppermute(block, axis, route)


def two_parts(matrix):
    high = matrix.astype(BF16)
    low = (matrix - high.astype(np.float64)).astype(BF16)
    return high, low


def transforms(rows, taps):
    size = rows + taps
    half = size // 2
    angle = 2 * np.pi * np.outer(np.arange(half), np.arange(size)) / size
    cosines = np.cos(angle)
    sines = -np.sin(angle)
    sines[0] = np.cos(np.pi * np.arange(size))
    forward = np.concatenate([cosines, sines], 0)
    weight = np.full((size, 1), 2.0 / size)
    weight[0] = weight[half] = 1.0 / size
    backward = (forward * weight).T
    f_high, f_low = two_parts(forward)
    b_high, b_low = two_parts(backward)
    cat = lambda *parts: np.concatenate(parts, 1)
    return (
        cat(f_high[:, :rows], f_low[:, :rows]),
        cat(f_high[:, :taps], f_low[:, :taps], f_high[:, :taps]),
        cat(f_high, f_low),
        cat(b_high, b_low),
    )


def dot(a, b):
    return jnp.dot(a, b, preferred_element_type=F32)


def chunk_terms(q_ext, k_ext, v_ext, up_ext, taps, weights, mats, rows, reach):
    to_mixed, to_taps, to_grad, back = mats
    size = up_ext.shape[0]
    half = size // 2

    def featured(ext, w, out_rows):
        total = w[0:1] * ext[PAD : PAD + out_rows, :]
        for j in range(1, reach):
            total += w[j : j + 1] * ext[PAD - j : PAD - j + out_rows, :]
        return total

    def lagged(grad, ext, out_rows):
        sums = [
            jnp.sum(grad * ext[PAD - j : PAD - j + out_rows, :], 0, keepdims=True)
            for j in range(reach)
        ]
        sums += [jnp.zeros_like(sums[0])] * (PAD - reach)
        return jnp.concatenate(sums, 0)

    key_part = featured(k_ext, weights[1], rows)
    value_part = featured(v_ext, weights[2], rows)
    mixed = (key_part * value_part).astype(BF16)
    m_hat = dot(to_mixed[...], jnp.concatenate([mixed, mixed], 0))
    taps_high = taps.astype(BF16)
    taps_low = (taps - taps_high.astype(F32)).astype(BF16)
    t_hat = dot(to_taps[...], jnp.concatenate([taps_high, taps_high, taps_low], 0))
    query = featured(q_ext, weights[0], size)
    grad_conv = (up_ext[...].astype(F32) * query).astype(BF16)
    g_hat = dot(to_grad[...], jnp.concatenate([grad_conv, grad_conv], 0))

    m_re, m_im = m_hat[:half], m_hat[half:]
    t_re, t_im = t_hat[:half], t_hat[half:]
    g_re, g_im = g_hat[:half], g_hat[half:]
    first = lax.broadcasted_iota(jnp.int32, m_re.shape, 0) == 0
    t_imz = jnp.where(first, 0.0, t_im)
    t_ren = jnp.where(first, t_im, t_re)
    m_imz = jnp.where(first, 0.0, m_im)
    m_ren = jnp.where(first, m_im, m_re)

    def inverse(re, im, out_rows):
        re, im = re.astype(BF16), im.astype(BF16)
        return dot(back[:out_rows, :], jnp.concatenate([re, im, re, im], 0))

    conv_out = inverse(
        m_re * t_re - m_im * t_imz, m_re * t_imz + m_im * t_ren, size
    )
    grad_mixed = inverse(
        g_re * t_re + g_im * t_imz, g_im * t_ren - g_re * t_imz, rows
    )
    filter_part = inverse(
        g_re * m_re + g_im * m_imz, g_im * m_ren - g_re * m_imz, taps.shape[0]
    )
    return (
        filter_part,
        lagged(up_ext[...].astype(F32) * conv_out, q_ext, size),
        lagged(grad_mixed * value_part, k_ext, rows),
        lagged(grad_mixed * key_part, v_ext, rows),
    )


def local_kernel(
    reach, xq, xk, xv, pq, pk, pv, nq, up, nup, taps, wq, wk, wv, m0, m1, m2, m3,
    filt, fq, fk, fv, q_ext, k_ext, v_ext, up_ext,
):
    rows = xq.shape[0]
    size = up_ext.shape[0]
    for ext, prev, block in ((q_ext, pq, xq), (k_ext, pk, xk), (v_ext, pv, xv)):
        ext[0:PAD, :] = prev[...].astype(F32)
        ext[PAD : PAD + rows, :] = block[...].astype(F32)
    q_ext[PAD + rows : PAD + size, :] = nq[...].astype(F32)
    up_ext[0:rows, :] = up[...]
    up_ext[rows:size, :] = nup[...]
    filt[...], fq[...], fk[...], fv[...] = chunk_terms(
        q_ext, k_ext, v_ext, up_ext, taps[...], (wq[...], wk[...], wv[...]),
        (m0, m1, m2, m3), rows, reach,
    )


def by_collectives(inputs, feat_weight, filter_taps, upstream):
    inputs_here = inputs[0]
    grad_here = upstream[0]
    rows = inputs_here.shape[0]
    channels = grad_here.shape[1]
    filt_rows = filter_taps.shape[0]
    reach = feat_weight.shape[0]
    scale = (lax.axis_size("dp") * lax.axis_size("ctx") * rows) ** (-0.5)
    feat_full, taps_full = (
        lax.all_gather(feat_weight, "dp", axis=1, tiled=True),
        lax.all_gather(filter_taps, "dp", axis=1, tiled=True),
    )
    next_grad, next_query = from_behind(
        (grad_here[:filt_rows], inputs_here[:filt_rows, :channels]), "ctx", -1
    )
    before = from_behind(inputs_here[rows - PAD :], "ctx", 1)
    weights = jnp.concatenate(
        [feat_full, jnp.zeros((PAD - reach, feat_full.shape[1]), F32)], 0
    )
    mats = [jnp.asarray(m) for m in transforms(rows, filt_rows)]
    width = 256
    steps = channels // width
    size = rows + filt_rows
    part = lambda r, group: pl.BlockSpec((r, width), lambda i: (0, i + group * steps))
    whole = lambda m: pl.BlockSpec(m.shape, lambda i: (0, 0))
    out = lambda r: jax.ShapeDtypeStruct((r, channels), F32)
    filter_part, feat_q, feat_k, feat_v = pl.pallas_call(
        functools.partial(local_kernel, reach),
        grid=(steps,),
        out_shape=[out(filt_rows), out(PAD), out(PAD), out(PAD)],
        in_specs=[part(rows, g) for g in range(3)]
        + [part(PAD, g) for g in range(3)]
        + [part(filt_rows, 0), part(rows, 0), part(filt_rows, 0), part(filt_rows, 0)]
        + [part(PAD, g) for g in range(3)]
        + [whole(m) for m in mats],
        out_specs=[part(filt_rows, 0)] + [part(PAD, 0)] * 3,
        scratch_shapes=[
            pltpu.VMEM((PAD + size, width), F32),
            pltpu.VMEM((PAD + rows, width), F32),
            pltpu.VMEM((PAD + rows, width), F32),
            pltpu.VMEM((size, width), BF16),
        ],
    )(
        inputs_here, inputs_here, inputs_here, before, before, before, next_query,
        grad_here, next_grad, taps_full, weights, weights, weights, *mats,
    )
    feat_part = jnp.concatenate([feat_q, feat_k, feat_v], 1)[:reach]
    filter_summed, feat_summed = (
        lax.psum_scatter(filter_part, "dp", scatter_dimension=1, tiled=True),
        lax.psum_scatter(feat_part, "dp", scatter_dimension=1, tiled=True),
    )
    filter_whole, feat_whole = lax.psum((filter_summed, feat_summed), "ctx")
    return (filter_whole * scale, feat_whole * scale)


MESH = pl.DeviceIdType.MESH
LANES = 128
PLANE = 4
TAIL = 16
AHEAD = 2


def fused_kernel(
    reach, x, up, taps_here, w_here, f0, f1, f2, f3, out,
    data, nxt, prev, taps_all, w_all, m0, m1, m2, m3, q_ext, k_ext, v_ext, up_ext,
    stage, dp_got, z_part, z_got, y_part, y_got, done, e_got,
    own_sem, fixed_sem, out_sem, swap_ssem, swap_rsem, x_ssem, x_rsem,
    nxt_ssem, nxt_rsem, tail_ssem, tail_rsem, dp_ssem, dp_rsem, z_ssem, z_rsem,
    y_ssem, y_rsem, e_ssem, e_rsem, ag_ssem, ag_rsem,
):
    n = lax.axis_size("ctx")
    me, core = lax.axis_index("ctx"), lax.axis_index("dp")
    side = lax.rem(me, 2)
    rows, channels = up.shape
    half = channels // 2
    filt_rows = taps_here.shape[0]
    chunks, planes = data.shape[1], z_got.shape[1]
    size = rows + filt_rows
    packed = stage.shape[2]
    level = me // PLANE
    partner = {"dp": 1 - core}
    across = {"ctx": me + 1 - 2 * side}
    beside = {"ctx": me + 2 - 4 * (lax.rem(me, PLANE) // 2)}
    before, after = {"ctx": lax.rem(me + n - 2, n)}, {"ctx": lax.rem(me + 2, n)}
    has_before, has_after = me >= 2, me < n - 2

    def column(k):
        return {"ctx": lax.rem(me + k * PLANE, n)}

    def plane_at(k):
        return lax.rem(level + k, planes)

    barrier = pltpu.get_barrier_semaphore()
    peers = [partner, across, before, after] + [column(k) for k in range(1, planes)]
    for peer in peers:
        pl.semaphore_signal(barrier, inc=1, device_id=peer, device_id_type=MESH)

    def local(src, dst, sem):
        return pltpu.make_async_copy(src, dst, sem)

    def remote(src, dst, send, got, device):
        return pltpu.make_async_remote_copy(
            src_ref=src, dst_ref=dst, send_sem=send, recv_sem=got,
            device_id=device, device_id_type=MESH,
        )

    def source(g, owner, c, p):
        low = (owner * chunks + c) * LANES + p * half + max(g - 1, 0) * channels
        at = pl.ds(pl.multiple_of(low, LANES), LANES)
        return x.at[:, at] if g else up.at[:, at]

    def place(owner, c, g, p):
        return data.at[owner, c, g, :, pl.ds(p * LANES, LANES)]

    def own_start(c):
        for g in range(4):
            for p in range(2):
                local(source(g, side, c, p), place(side, c, g, p), own_sem.at[c]).start()

    def own_wait(c):
        local(data.at[1 - side, c], data.at[side, c], own_sem.at[c]).wait()

    def x_start(c):
        for g in range(4):
            for p in range(2):
                remote(
                    source(g, 1 - side, c, p), place(side, c, g, p),
                    x_ssem.at[c, g // 2], x_rsem.at[c, g // 2], across,
                ).start()

    def x_whole(c, part):
        block = data.at[1 - side, c, pl.ds(2 * part, 2)]
        return remote(block, block, x_ssem.at[c, part], x_rsem.at[c, part], across)

    def nxt_copy(c):
        return remote(
            data.at[0, c, pl.ds(0, 2)], nxt.at[c], nxt_ssem.at[c], nxt_rsem.at[c], before
        )

    def tail_copy(c):
        return remote(
            data.at[1, c, pl.ds(1, 3), pl.ds(rows - TAIL, TAIL)], prev.at[c],
            tail_ssem.at[c], tail_rsem.at[c], after,
        )

    def dp_copy(c):
        return remote(
            stage.at[c, 1 - core], dp_got.at[c], dp_ssem.at[c], dp_rsem.at[c], partner
        )

    def z_copy(c, k):
        return remote(
            z_part.at[c, plane_at(k)], z_got.at[c, level], z_ssem.at[c, k],
            z_rsem.at[c, level], column(k),
        )

    def z_arrival(c, k):
        return remote(
            z_part.at[c, 0], z_got.at[c, plane_at(k)], z_ssem.at[c, k],
            z_rsem.at[c, plane_at(k)], column(k),
        )

    def y_copy(c):
        return remote(y_part.at[c], y_got.at[c], y_ssem.at[c], y_rsem.at[c], beside)

    def e_copy(c):
        return remote(done.at[c], e_got.at[c], e_ssem.at[c], e_rsem.at[c], across)

    def ag_copy(c, foreign, k):
        owner = (side + foreign - 2 * side * foreign) * chunks + c
        return remote(
            (e_got if foreign else done).at[c], out.at[owner, level],
            ag_ssem.at[c, foreign, k], ag_rsem.at[owner, level], column(k),
        )

    def ag_arrival(owner, k):
        return remote(
            done.at[0], out.at[owner, plane_at(k)], ag_ssem.at[0, 0, k],
            ag_rsem.at[owner, plane_at(k)], column(k),
        )

    def out_copy(c, foreign):
        owner = (side + foreign - 2 * side * foreign) * chunks + c
        return local(
            (e_got if foreign else done).at[c], out.at[owner, level], out_sem.at[c, foreign]
        )

    taps_side = pl.ds(pl.multiple_of(side * chunks * LANES, LANES), chunks * LANES)
    swaps = (
        remote(taps_here.at[:, taps_side], taps_all.at[core], swap_ssem.at[0], swap_rsem.at[0], partner),
        remote(w_here, w_all.at[core], swap_ssem.at[1], swap_rsem.at[1], partner),
    )
    kept = [
        local(taps_here.at[:, taps_side], taps_all.at[core], fixed_sem.at[0]),
        local(w_here, w_all.at[core], fixed_sem.at[1]),
    ] + [local(f, m, fixed_sem.at[2 + i]) for i, (f, m) in enumerate(((f0, m0), (f1, m1), (f2, m2), (f3, m3)))]

    own_start(0)
    for copy in kept:
        copy.start()

    @pl.loop(1, chunks)
    def _(c):
        own_start(c)

    pl.semaphore_wait(barrier, len(peers))

    @pl.loop(0, AHEAD)
    def _(c):
        x_start(c)

    for copy in swaps:
        copy.start()

    @pl.when(me < 2)
    def _():
        prev[...] = jnp.zeros_like(prev)

    @pl.when(me >= n - 2)
    def _():
        nxt[...] = jnp.zeros_like(nxt)

    for copy in kept:
        copy.wait()
    own_wait(0)

    @pl.when((side == 0) & has_before)
    def _():
        nxt_copy(0).start()

    @pl.when((side == 1) & has_after)
    def _():
        tail_copy(0).start()

    for copy in swaps:
        copy.wait()

    def block_terms(c, b, taps, weights):
        old = prev[c].astype(F32) if b == 0 else data[0, c, 1:4, rows - TAIL :, :].astype(F32)
        for g, ext in enumerate((q_ext, k_ext, v_ext)):
            ext[0:PAD, :] = old[g, TAIL - PAD :]
            ext[PAD : PAD + rows, :] = data[b, c, g + 1].astype(F32)
        ahead = (data[1, c, 0], data[1, c, 1]) if b == 0 else (nxt[c, 0], nxt[c, 1])
        q_ext[PAD + rows : PAD + size, :] = ahead[1].astype(F32)
        up_ext[0:rows, :] = data[b, c, 0]
        up_ext[rows:size, :] = ahead[0]
        return chunk_terms(
            q_ext, k_ext, v_ext, up_ext, taps, weights, (m0, m1, m2, m3), rows, reach
        )

    def compute(c):
        @pl.when(c + AHEAD < chunks)
        def _():
            x_start(c + AHEAD)

        @pl.when(c + 1 < chunks)
        def _():
            own_wait(c + 1)

        @pl.when((side == 0) & has_before & (c + 1 < chunks))
        def _():
            nxt_copy(c + 1).start()

        @pl.when((side == 1) & has_after & (c + 1 < chunks))
        def _():
            tail_copy(c + 1).start()

        x_whole(c, 0).wait_recv()

        @pl.when((side == 1) & has_before)
        def _():
            nxt_copy(c).start()

        x_whole(c, 1).wait_recv()

        @pl.when((side == 0) & has_after)
        def _():
            tail_copy(c).start()

        @pl.when(has_before)
        def _():
            tail_copy(c).wait_recv()

        here = pl.ds(pl.multiple_of(c * LANES, LANES), LANES)
        taps = jnp.concatenate([taps_all[p, :, here] for p in range(2)], 1)

        def weight(g, p):
            part, slot = divmod(2 * g + p, 3)
            low = (side * chunks + c) * LANES + slot * half
            return w_all[part, :, pl.ds(pl.multiple_of(low, LANES), LANES)]

        weights = [jnp.concatenate([weight(g, p) for p in range(2)], 1) for g in range(3)]
        first = block_terms(c, 0, taps, weights)

        @pl.when(has_after)
        def _():
            nxt_copy(c).wait_recv()

        second = block_terms(c, 1, taps, weights)
        filt, feat_q, feat_k, feat_v = [a + b for a, b in zip(first, second)]
        a, b = slice(0, LANES), slice(LANES, 2 * LANES)
        rest = [jnp.zeros((packed - filt_rows - 3 * PAD, LANES), F32)]
        stage[c, 0] = jnp.concatenate(
            [filt[:, a], feat_q[:, a], feat_q[:, b], feat_k[:, a]] + rest, 0
        )
        stage[c, 1] = jnp.concatenate(
            [filt[:, b], feat_k[:, b], feat_v[:, a], feat_v[:, b]] + rest, 0
        )
        dp_copy(c).start()

    def along_z(c):
        dp_copy(c).wait_recv()
        pair = stage[c, core] + dp_got[c]
        z_part[c] = pair.reshape(planes, packed // planes, LANES)
        for k in range(1, planes):
            z_copy(c, k).start()

    def along_y(c):
        total = z_part[c, level]
        for k in range(1, planes):
            z_arrival(c, k).wait_recv()
            total += z_got[c, plane_at(k)]
        y_part[c] = total
        y_copy(c).start()

    def share(c, foreign):
        for k in range(1, planes):
            ag_copy(c, foreign, k).start()
        out_copy(c, foreign).start()

    def along_x(c):
        y_copy(c).wait_recv()
        done[c] = (y_part[c] + y_got[c]).astype(BF16)
        e_copy(c).start()
        share(c, 0)

    def finish(c):
        e_copy(c).wait_recv()
        share(c, 1)

    steps = ((compute, 0), (along_z, 1), (along_y, 2), (along_x, 3), (finish, 5))

    @pl.loop(0, chunks + steps[-1][1])
    def _(i):
        for step, lag in steps:
            @pl.when((i >= lag) & (i - lag < chunks))
            def _():
                step(i - lag)

    @pl.loop(0, chunks)
    def _(c):
        for k in range(1, planes):
            ag_arrival(c, k).wait_recv()
            ag_arrival(c + chunks, k).wait_recv()
        for foreign in range(2):
            out_copy(c, foreign).wait()
            for k in range(1, planes):
                ag_copy(c, foreign, k).wait_send()
        for part in range(2):
            x_whole(c, part).wait_send()
        dp_copy(c).wait_send()
        for k in range(1, planes):
            z_copy(c, k).wait_send()
        y_copy(c).wait_send()
        e_copy(c).wait_send()

    @pl.when(has_before)
    def _():
        @pl.loop(0, chunks)
        def _(c):
            nxt_copy(c).wait_send()

    @pl.when(has_after)
    def _():
        @pl.loop(0, chunks)
        def _(c):
            tail_copy(c).wait_send()


def unpack_kernel(scale, reach, got, filt, feat):
    filt_rows = filt.shape[0]
    half = got.shape[0] * LANES
    for owner in range(got.shape[0]):
        value = got[owner].astype(F32).reshape(-1, LANES) * scale
        filt[:, owner * LANES : (owner + 1) * LANES] = value[:filt_rows]
        for g in range(3):
            low = filt_rows + g * PAD
            at = owner * LANES + g * half
            feat[:, at : at + LANES] = value[low : low + reach]


def fused(inputs, feat_weight, filter_taps, upstream):
    x, up = inputs[0], upstream[0]
    n = lax.axis_size("ctx")
    rows, channels = up.shape
    filt_rows, reach = filter_taps.shape[0], feat_weight.shape[0]
    scale = (lax.axis_size("dp") * n * rows) ** (-0.5)
    mats = [jnp.asarray(m) for m in transforms(rows, filt_rows)]
    size = rows + filt_rows
    width = 2 * LANES
    chunks = channels // (2 * width)
    planes = n // PLANE
    packed = -(-(filt_rows + 3 * PAD) // (planes * PAD)) * (planes * PAD)
    cut = packed // planes
    dma = lambda *shape: pltpu.SemaphoreType.DMA(shape)
    anywhere = pl.BlockSpec(memory_space=pl.ANY)
    gathered = pl.pallas_call(
        functools.partial(fused_kernel, reach),
        out_shape=jax.ShapeDtypeStruct((2 * chunks, planes, cut, LANES), BF16),
        in_specs=[anywhere] * 8,
        out_specs=anywhere,
        scratch_shapes=[
            pltpu.VMEM((2, chunks, 4, rows, width), BF16),
            pltpu.VMEM((chunks, 2, rows, width), BF16),
            pltpu.VMEM((chunks, 3, TAIL, width), BF16),
            pltpu.VMEM((2, filt_rows, chunks * LANES), F32),
            pltpu.VMEM((2,) + feat_weight.shape, F32),
            *[pltpu.VMEM(m.shape, BF16) for m in mats],
            pltpu.VMEM((PAD + size, width), F32),
            pltpu.VMEM((PAD + rows, width), F32),
            pltpu.VMEM((PAD + rows, width), F32),
            pltpu.VMEM((size, width), BF16),
            pltpu.VMEM((chunks, 2, packed, LANES), F32),
            pltpu.VMEM((chunks, packed, LANES), F32),
            pltpu.VMEM((chunks, planes, cut, LANES), F32),
            pltpu.VMEM((chunks, planes, cut, LANES), F32),
            pltpu.VMEM((chunks, cut, LANES), F32),
            pltpu.VMEM((chunks, cut, LANES), F32),
            pltpu.VMEM((chunks, cut, LANES), BF16),
            pltpu.VMEM((chunks, cut, LANES), BF16),
            dma(chunks), dma(6), dma(chunks, 2), dma(2), dma(2),
            dma(chunks, 2), dma(chunks, 2),
            *[dma(chunks)] * 6,
            dma(chunks, planes), dma(chunks, planes),
            *[dma(chunks)] * 4,
            dma(chunks, 2, planes), dma(2 * chunks, planes),
        ],
        compiler_params=pltpu.CompilerParams(
            collective_id=0, has_side_effects=True, vmem_limit_bytes=63 * 2**20
        ),
    )(x, up, filter_taps, feat_weight, *mats)
    return pl.pallas_call(
        functools.partial(unpack_kernel, scale, reach),
        out_shape=[
            jax.ShapeDtypeStruct(filter_taps.shape, F32),
            jax.ShapeDtypeStruct(feat_weight.shape, F32),
        ],
        in_specs=[pl.BlockSpec(memory_space=pltpu.VMEM)],
        out_specs=[pl.BlockSpec(memory_space=pltpu.VMEM)] * 2,
    )(gathered)


def per_device(inputs, feat_weight, filter_taps, upstream):
    n = lax.axis_size("ctx")
    rows, channels = upstream.shape[1:]
    whole = n % PLANE == 0 and n // PLANE > 1 and channels == 2 * n * LANES
    square = rows == filter_taps.shape[0] and feat_weight.shape[0] <= PAD
    if lax.axis_size("dp") == 2 and whole and square and rows % TAIL == 0:
        return fused(inputs, feat_weight, filter_taps, upstream)
    return by_collectives(inputs, feat_weight, filter_taps, upstream)


def solution(mesh):
    placed = (P("dp", "ctx", None), P(None, "dp"), P(None, "dp"), P("dp", "ctx", None))
    return jax.shard_map(
        per_device,
        mesh=mesh,
        in_specs=placed,
        out_specs=(P(None, "dp"), P(None, "dp")),
        check_vma=False,
    )
```

time: 97.1 us -> 90.6 us (0.933); the launches traced: 96.9 us -> 88.8 us
  Pallas kernels: 92.4 us -> 88.2 us
  local copies, waits for them, and re-layouts: 3.91 us -> 0 us
    pallas_call x1 -> x2, Pallas kernels: 92.4 us -> 88.2 us  [the longest x1 85.9 us: fused(): pl.pallas_call(functools.partial(fused_kernel, reach), out_shape=jax.Shap...]
    unnamed x2 -> x0, local copies, waits for them, and re-layouts: 3.91 us -> none
where the time goes in v1:
time: 90.6 us; the launch traced here: 88.8 us
  Pallas kernels  88.2 us (97%)
    pallas_call x1, Pallas kernels, fused(): pl.pallas_call(functools.partial(fused_kernel, reach), out_shape=jax.Shap...  85.9 us
    pallas_call x1, Pallas kernels, fused(): pl.pallas_call(functools.partial(unpack_kernel, scale, reach), out_shape=...  2.24 us

profile of v1, /device:TPU:0, one launch (start us, length us, event | category | flops | bytes accessed | tf_op | source)
XLA Modules:
  0.0 88.8 jit_solution(1279881529654989531)
XLA Ops:
  0.6 85.9 %shard_map.95.got = bf16[16,4,40,128]{3,2,1,0:T(8,128)(2,1)} custom-call(bf16[128,12288]{1,0:T(8,128)(2,1)} %bitcast.2, bf16[128,4096]{1,0:T(8,128)(2,1)} %bitcast.3, f32[128,2048]{1,0:T(8,128)} %taps_here.1, f32[7,6144]{1,0:T(8,128)} %w_here.1, bf16[256,256]{1,0:T(8,128)(2,1)} %constant.8.clone.f0, bf16[256,384]{1,0:T(8,128)(2,1)} %constant.9.clone.f1, ...), custom_call_target="tpu_custom_call" | custom-call | tf_op jit(solution)/shard_map/pallas_call | solution.py:538
  86.5 2.2 %shard_map.96 = (f32[128,2048]{1,0:T(8,128)}, f32[7,6144]{1,0:T(8,128)}) custom-call(bf16[16,4,40,128]{3,2,1,0:T(8,128)(2,1)} %shard_map.95.got), custom_call_target="tpu_custom_call" | custom-call | tf_op jit(solution)/shard_map/pallas_call | solution.py:573

commit v2 on v1

--- a/solution.py
+++ b/solution.py
@@ -51,8 +51,19 @@
     return jnp.dot(a, b, preferred_element_type=F32)
 
 
-def chunk_terms(q_ext, k_ext, v_ext, up_ext, taps, weights, mats, rows, reach):
-    to_mixed, to_taps, to_grad, back = mats
+def taps_transform(taps, to_taps):
+    taps_high = taps.astype(BF16)
+    taps_low = (taps - taps_high.astype(F32)).astype(BF16)
+    return dot(to_taps[...], jnp.concatenate([taps_high, taps_high, taps_low], 0))
+
+
+def inverse(re, im, back, out_rows):
+    re, im = re.astype(BF16), im.astype(BF16)
+    return dot(back[:out_rows, :], jnp.concatenate([re, im, re, im], 0))
+
+
+def chunk_terms(q_ext, k_ext, v_ext, up_ext, t_hat, weights, mats, rows, reach):
+    to_mixed, to_grad, back = mats
     size = up_ext.shape[0]
     half = size // 2
 
@@ -74,9 +85,6 @@
     value_part = featured(v_ext, weights[2], rows)
     mixed = (key_part * value_part).astype(BF16)
     m_hat = dot(to_mixed[...], jnp.concatenate([mixed, mixed], 0))
-    taps_high = taps.astype(BF16)
-    taps_low = (taps - taps_high.astype(F32)).astype(BF16)
-    t_hat = dot(to_taps[...], jnp.concatenate([taps_high, taps_high, taps_low], 0))
     query = featured(q_ext, weights[0], size)
     grad_conv = (up_ext[...].astype(F32) * query).astype(BF16)
     g_hat = dot(to_grad[...], jnp.concatenate([grad_conv, grad_conv], 0))
@@ -90,21 +98,15 @@
     m_imz = jnp.where(first, 0.0, m_im)
     m_ren = jnp.where(first, m_im, m_re)
 
-    def inverse(re, im, out_rows):
-        re, im = re.astype(BF16), im.astype(BF16)
-        return dot(back[:out_rows, :], jnp.concatenate([re, im, re, im], 0))
-
     conv_out = inverse(
-        m_re * t_re - m_im * t_imz, m_re * t_imz + m_im * t_ren, size
+        m_re * t_re - m_im * t_imz, m_re * t_imz + m_im * t_ren, back, size
     )
     grad_mixed = inverse(
-        g_re * t_re + g_im * t_imz, g_im * t_ren - g_re * t_imz, rows
-    )
-    filter_part = inverse(
-        g_re * m_re + g_im * m_imz, g_im * m_ren - g_re * m_imz, taps.shape[0]
+        g_re * t_re + g_im * t_imz, g_im * t_ren - g_re * t_imz, back, rows
     )
     return (
-        filter_part,
+        g_re * m_re + g_im * m_imz,
+        g_im * m_ren - g_re * m_imz,
         lagged(up_ext[...].astype(F32) * conv_out, q_ext, size),
         lagged(grad_mixed * value_part, k_ext, rows),
         lagged(grad_mixed * key_part, v_ext, rows),
@@ -123,10 +125,12 @@
     q_ext[PAD + rows : PAD + size, :] = nq[...].astype(F32)
     up_ext[0:rows, :] = up[...]
     up_ext[rows:size, :] = nup[...]
-    filt[...], fq[...], fk[...], fv[...] = chunk_terms(
-        q_ext, k_ext, v_ext, up_ext, taps[...], (wq[...], wk[...], wv[...]),
-        (m0, m1, m2, m3), rows, reach,
-    )
+    t_hat = taps_transform(taps[...], m1)
+    cross_re, cross_im, fq[...], fk[...], fv[...] = chunk_terms(
+        q_ext, k_ext, v_ext, up_ext, t_hat, (wq[...], wk[...], wv[...]),
+        (m0, m2, m3), rows, reach,
+    )
+    filt[...] = inverse(cross_re, cross_im, m3, taps.shape[0])
 
 
 def by_collectives(inputs, feat_weight, filter_taps, upstream):
@@ -193,7 +197,7 @@
 
 def fused_kernel(
     reach, x, up, taps_here, w_here, f0, f1, f2, f3, out,
-    data, nxt, prev, taps_all, w_all, m0, m1, m2, m3, q_ext, k_ext, v_ext, up_ext,
+    data, prev, taps_all, w_all, m0, m1, m2, m3, q_ext, k_ext, v_ext, up_ext,
     stage, dp_got, z_part, z_got, y_part, y_got, done, e_got,
     own_sem, fixed_sem, out_sem, swap_ssem, swap_rsem, x_ssem, x_rsem,
     nxt_ssem, nxt_rsem, tail_ssem, tail_rsem, dp_ssem, dp_rsem, z_ssem, z_rsem,
@@ -265,7 +269,7 @@
 
     def nxt_copy(c):
         return remote(
-            data.at[0, c, pl.ds(0, 2)], nxt.at[c], nxt_ssem.at[c], nxt_rsem.at[c], before
+            data.at[0, c, pl.ds(0, 2)], data.at[2, c, pl.ds(0, 2)], nxt_ssem.at[c], nxt_rsem.at[c], before
         )
 
     def tail_copy(c):
@@ -349,7 +353,7 @@
 
     @pl.when(me >= n - 2)
     def _():
-        nxt[...] = jnp.zeros_like(nxt)
+        data[2, :, 0:2] = jnp.zeros_like(data[2, :, 0:2])
 
     for copy in kept:
         copy.wait()
@@ -366,17 +370,26 @@
     for copy in swaps:
         copy.wait()
 
-    def block_terms(c, b, taps, weights):
-        old = prev[c].astype(F32) if b == 0 else data[0, c, 1:4, rows - TAIL :, :].astype(F32)
+    def block_terms(c, b, t_hat, weights):
+        def start(old):
+            for g, ext in enumerate((q_ext, k_ext, v_ext)):
+                ext[0:PAD, :] = old[g].astype(F32)[TAIL - PAD :]
+
+        @pl.when(b == 0)
+        def _():
+            start(prev[c])
+
+        @pl.when(b == 1)
+        def _():
+            start(data[0, c, 1:4, rows - TAIL :, :])
+
         for g, ext in enumerate((q_ext, k_ext, v_ext)):
-            ext[0:PAD, :] = old[g, TAIL - PAD :]
             ext[PAD : PAD + rows, :] = data[b, c, g + 1].astype(F32)
-        ahead = (data[1, c, 0], data[1, c, 1]) if b == 0 else (nxt[c, 0], nxt[c, 1])
-        q_ext[PAD + rows : PAD + size, :] = ahead[1].astype(F32)
+        q_ext[PAD + rows : PAD + size, :] = data[b + 1, c, 1].astype(F32)
         up_ext[0:rows, :] = data[b, c, 0]
-        up_ext[rows:size, :] = ahead[0]
+        up_ext[rows:size, :] = data[b + 1, c, 0]
         return chunk_terms(
-            q_ext, k_ext, v_ext, up_ext, taps, weights, (m0, m1, m2, m3), rows, reach
+            q_ext, k_ext, v_ext, up_ext, t_hat, weights, (m0, m2, m3), rows, reach
         )
 
     def compute(c):
@@ -408,7 +421,11 @@
         def _():
             tail_copy(c).start()
 
-        @pl.when(has_before)
+        @pl.when((side == 0) & has_after)
+        def _():
+            nxt_copy(c).wait_recv()
+
+        @pl.when((side == 1) & has_before)
         def _():
             tail_copy(c).wait_recv()
 
@@ -421,14 +438,20 @@
             return w_all[part, :, pl.ds(pl.multiple_of(low, LANES), LANES)]
 
         weights = [jnp.concatenate([weight(g, p) for p in range(2)], 1) for g in range(3)]
-        first = block_terms(c, 0, taps, weights)
-
-        @pl.when(has_after)
+        t_hat = taps_transform(taps, m1)
+        first = block_terms(c, 1 - side, t_hat, weights)
+
+        @pl.when((side == 0) & has_before)
+        def _():
+            tail_copy(c).wait_recv()
+
+        @pl.when((side == 1) & has_after)
         def _():
             nxt_copy(c).wait_recv()
 
-        second = block_terms(c, 1, taps, weights)
-        filt, feat_q, feat_k, feat_v = [a + b for a, b in zip(first, second)]
+        second = block_terms(c, side, t_hat, weights)
+        cross_re, cross_im, feat_q, feat_k, feat_v = [a + b for a, b in zip(first, second)]
+        filt = inverse(cross_re, cross_im, m3, filt_rows)
         a, b = slice(0, LANES), slice(LANES, 2 * LANES)
         rest = [jnp.zeros((packed - filt_rows - 3 * PAD, LANES), F32)]
         stage[c, 0] = jnp.concatenate(
@@ -442,15 +465,17 @@
     def along_z(c):
         dp_copy(c).wait_recv()
         pair = stage[c, core] + dp_got[c]
-        z_part[c] = pair.reshape(planes, packed // planes, LANES)
+        z_part[c] = pair.reshape(planes, packed // planes, LANES).astype(BF16)
         for k in range(1, planes):
             z_copy(c, k).start()
 
     def along_y(c):
-        total = z_part[c, level]
+        cut = packed // planes
+        mine = pl.ds(pl.multiple_of(level * cut, PAD), cut)
+        total = stage[c, core, mine] + dp_got[c, mine]
         for k in range(1, planes):
             z_arrival(c, k).wait_recv()
-            total += z_got[c, plane_at(k)]
+            total += z_got[c, plane_at(k)].astype(F32)
         y_part[c] = total
         y_copy(c).start()
 
@@ -541,8 +566,7 @@
         in_specs=[anywhere] * 8,
         out_specs=anywhere,
         scratch_shapes=[
-            pltpu.VMEM((2, chunks, 4, rows, width), BF16),
-            pltpu.VMEM((chunks, 2, rows, width), BF16),
+            pltpu.VMEM((3, chunks, 4, rows, width), BF16),
             pltpu.VMEM((chunks, 3, TAIL, width), BF16),
             pltpu.VMEM((2, filt_rows, chunks * LANES), F32),
             pltpu.VMEM((2,) + feat_weight.shape, F32),
@@ -553,8 +577,8 @@
             pltpu.VMEM((size, width), BF16),
             pltpu.VMEM((chunks, 2, packed, LANES), F32),
             pltpu.VMEM((chunks, packed, LANES), F32),
-            pltpu.VMEM((chunks, planes, cut, LANES), F32),
-            pltpu.VMEM((chunks, planes, cut, LANES), F32),
+            pltpu.VMEM((chunks, planes, cut, LANES), BF16),
+            pltpu.VMEM((chunks, planes, cut, LANES), BF16),
             pltpu.VMEM((chunks, cut, LANES), F32),
             pltpu.VMEM((chunks, cut, LANES), F32),
             pltpu.VMEM((chunks, cut, LANES), BF16),

time: 90.6 us -> 82.3 us (0.908); the launches traced: 88.8 us -> 82.1 us
  Pallas kernels: 88.2 us -> 81.5 us
    pallas_call x1, Pallas kernels: 85.9 us -> 79.2 us  [fused(): pl.pallas_call(functools.partial(fused_kernel, reach), out_shape=jax.Shap...]
where the time goes in v2:
time: 82.3 us; the launch traced here: 82.1 us
  Pallas kernels  81.5 us (99%)
    pallas_call x1, Pallas kernels, fused(): pl.pallas_call(functools.partial(fused_kernel, reach), out_shape=jax.Shap...  79.2 us
    pallas_call x1, Pallas kernels, fused(): pl.pallas_call(functools.partial(unpack_kernel, scale, reach), out_shape=...  2.24 us

profile of v2, /device:TPU:0, one launch (start us, length us, event | category | flops | bytes accessed | tf_op | source)
XLA Modules:
  0.0 82.1 jit_solution(2227176410640869256)
XLA Ops:
  0.6 79.2 %shard_map.95.got = bf16[16,4,40,128]{3,2,1,0:T(8,128)(2,1)} custom-call(bf16[128,12288]{1,0:T(8,128)(2,1)} %bitcast.2, bf16[128,4096]{1,0:T(8,128)(2,1)} %bitcast.3, f32[128,2048]{1,0:T(8,128)} %taps_here.1, f32[7,6144]{1,0:T(8,128)} %w_here.1, bf16[256,256]{1,0:T(8,128)(2,1)} %constant.8.clone.f0, bf16[256,384]{1,0:T(8,128)(2,1)} %constant.9.clone.f1, ...), custom_call_target="tpu_custom_call" | custom-call | tf_op jit(solution)/shard_map/pallas_call | solution.py:563
  79.9 2.2 %shard_map.96 = (f32[128,2048]{1,0:T(8,128)}, f32[7,6144]{1,0:T(8,128)}) custom-call(bf16[16,4,40,128]{3,2,1,0:T(8,128)(2,1)} %shard_map.95.got), custom_call_target="tpu_custom_call" | custom-call | tf_op jit(solution)/shard_map/pallas_call | solution.py:597

commit v3 on v2

--- a/solution.py
+++ b/solution.py
@@ -193,6 +193,7 @@
 PLANE = 4
 TAIL = 16
 AHEAD = 2
+LATE = 3
 
 
 def fused_kernel(
@@ -225,8 +226,13 @@
     def plane_at(k):
         return lax.rem(level + k, planes)
 
+    def over(k):
+        return {"ctx": lax.rem(me + 1 - 2 * side + n + k * PLANE, n)}
+
+    early = chunks - LATE
     barrier = pltpu.get_barrier_semaphore()
-    peers = [partner, across, before, after] + [column(k) for k in range(1, planes)]
+    peers = [partner, across, before, after]
+    peers += [far(k) for k in range(1, planes) for far in (column, over)]
     for peer in peers:
         pl.semaphore_signal(barrier, inc=1, device_id=peer, device_id_type=MESH)
 
@@ -255,12 +261,12 @@
     def own_wait(c):
         local(data.at[1 - side, c], data.at[side, c], own_sem.at[c]).wait()
 
-    def x_start(c):
-        for g in range(4):
+    def x_start(c, part):
+        for g in range(2 * part, 2 * part + 2):
             for p in range(2):
                 remote(
                     source(g, 1 - side, c, p), place(side, c, g, p),
-                    x_ssem.at[c, g // 2], x_rsem.at[c, g // 2], across,
+                    x_ssem.at[c, part], x_rsem.at[c, part], across,
                 ).start()
 
     def x_whole(c, part):
@@ -311,7 +317,14 @@
     def ag_arrival(owner, k):
         return remote(
             done.at[0], out.at[owner, plane_at(k)], ag_ssem.at[0, 0, k],
-            ag_rsem.at[owner, plane_at(k)], column(k),
+            ag_rsem.at[owner, plane_at(k)], across,
+        )
+
+    def over_copy(c, k):
+        owner = side * chunks + c
+        return remote(
+            done.at[c], out.at[owner, level], ag_ssem.at[c, 1, k], ag_rsem.at[owner, level],
+            over(k),
         )
 
     def out_copy(c, foreign):
@@ -340,9 +353,12 @@
 
     pl.semaphore_wait(barrier, len(peers))
 
+    x_start(0, 0)
+
     @pl.loop(0, AHEAD)
     def _(c):
-        x_start(c)
+        x_start(c + 1, 0)
+        x_start(c, 1)
 
     for copy in swaps:
         copy.start()
@@ -369,6 +385,12 @@
 
     for copy in swaps:
         copy.wait()
+
+    x_whole(0, 0).wait_recv()
+
+    @pl.when((side == 1) & has_before)
+    def _():
+        nxt_copy(0).start()
 
     def block_terms(c, b, t_hat, weights):
         def start(old):
@@ -393,9 +415,13 @@
         )
 
     def compute(c):
+        @pl.when(c + AHEAD + 1 < chunks)
+        def _():
+            x_start(c + AHEAD + 1, 0)
+
         @pl.when(c + AHEAD < chunks)
         def _():
-            x_start(c + AHEAD)
+            x_start(c + AHEAD, 1)
 
         @pl.when(c + 1 < chunks)
         def _():
@@ -409,11 +435,13 @@
         def _():
             tail_copy(c + 1).start()
 
-        x_whole(c, 0).wait_recv()
-
-        @pl.when((side == 1) & has_before)
-        def _():
-            nxt_copy(c).start()
+        @pl.when(c + 1 < chunks)
+        def _():
+            x_whole(c + 1, 0).wait_recv()
+
+        @pl.when((side == 1) & has_before & (c + 1 < chunks))
+        def _():
+            nxt_copy(c + 1).start()
 
         x_whole(c, 1).wait_recv()
 
@@ -487,12 +515,22 @@
     def along_x(c):
         y_copy(c).wait_recv()
         done[c] = (y_part[c] + y_got[c]).astype(BF16)
-        e_copy(c).start()
+        @pl.when(c < early)
+        def _():
+            e_copy(c).start()
+
+        @pl.when(c >= early)
+        def _():
+            for k in range(planes):
+                over_copy(c, k).start()
+
         share(c, 0)
 
     def finish(c):
-        e_copy(c).wait_recv()
-        share(c, 1)
+        @pl.when(c < early)
+        def _():
+            e_copy(c).wait_recv()
+            share(c, 1)
 
     steps = ((compute, 0), (along_z, 1), (along_y, 2), (along_x, 3), (finish, 5))
 
@@ -508,17 +546,29 @@
         for k in range(1, planes):
             ag_arrival(c, k).wait_recv()
             ag_arrival(c + chunks, k).wait_recv()
-        for foreign in range(2):
-            out_copy(c, foreign).wait()
+        out_copy(c, 0).wait()
+        for k in range(1, planes):
+            ag_copy(c, 0, k).wait_send()
+
+        @pl.when(c < early)
+        def _():
+            e_copy(c).wait_send()
+            out_copy(c, 1).wait()
             for k in range(1, planes):
-                ag_copy(c, foreign, k).wait_send()
+                ag_copy(c, 1, k).wait_send()
+
+        @pl.when(c >= early)
+        def _():
+            ag_arrival((1 - side) * chunks + c, 0).wait_recv()
+            for k in range(planes):
+                over_copy(c, k).wait_send()
+
         for part in range(2):
             x_whole(c, part).wait_send()
         dp_copy(c).wait_send()
         for k in range(1, planes):
             z_copy(c, k).wait_send()
         y_copy(c).wait_send()
-        e_copy(c).wait_send()
 
     @pl.when(has_before)
     def _():

time: 82.3 us -> 80.4 us (0.977)
  Pallas kernels: 81.5 us -> 79.6 us
    pallas_call x1, Pallas kernels: 79.2 us -> 77.4 us  [fused(): pl.pallas_call(functools.partial(fused_kernel, reach), out_shape=jax.Shap...]
where the time goes in v3:
time: 80.4 us; the launch traced here: 80.2 us
  Pallas kernels  79.6 us (99%)
    pallas_call x1, Pallas kernels, fused(): pl.pallas_call(functools.partial(fused_kernel, reach), out_shape=jax.Shap...  77.4 us
    pallas_call x1, Pallas kernels, fused(): pl.pallas_call(functools.partial(unpack_kernel, scale, reach), out_shape=...  2.24 us

profile of v3, /device:TPU:0, one launch (start us, length us, event | category | flops | bytes accessed | tf_op | source)
XLA Modules:
  0.0 80.2 jit_solution(2088058793819512528)
XLA Ops:
  0.6 77.4 %shard_map.95.got = bf16[16,4,40,128]{3,2,1,0:T(8,128)(2,1)} custom-call(bf16[128,12288]{1,0:T(8,128)(2,1)} %bitcast.2, bf16[128,4096]{1,0:T(8,128)(2,1)} %bitcast.3, f32[128,2048]{1,0:T(8,128)} %taps_here.1, f32[7,6144]{1,0:T(8,128)} %w_here.1, bf16[256,256]{1,0:T(8,128)(2,1)} %constant.8.clone.f0, bf16[256,384]{1,0:T(8,128)(2,1)} %constant.9.clone.f1, ...), custom_call_target="tpu_custom_call" | custom-call | tf_op jit(solution)/shard_map/pallas_call | solution.py:613
  78.0 2.2 %shard_map.96 = (f32[128,2048]{1,0:T(8,128)}, f32[7,6144]{1,0:T(8,128)}) custom-call(bf16[16,4,40,128]{3,2,1,0:T(8,128)(2,1)} %shard_map.95.got), custom_call_target="tpu_custom_call" | custom-call | tf_op jit(solution)/shard_map/pallas_call | solution.py:647
